TPU v7x, 256 devices: a whole 4x4x8 slice. The times are simulated.
256 devices in a mesh: dp: 32 (over y, x, core), tsp: 8 (over z).
Axes of the slice: x: 4, y: 4, z: 8, core: 2. Of those that a mesh axis runs over, the one named last changes fastest.
Arguments:
- tokens: bfloat16 [65536, 8192], P('dp', 'tsp'), may hold values from -6 to 6
- cotangent: bfloat16 [65536, 1024], P('dp', 'tsp'), may hold values from -6 to 6
- frozen_key_weight: bfloat16 [8192, 1024], P('tsp'), may hold values from -0.1875 to 0.1875
- adapter_down_weight: bfloat16 [64, 64, 8192], P('dp', None, 'tsp'), may hold values from -0.0625 to 0.0625
- adapter_up_weight: bfloat16 [64, 64, 1024], P('dp', None, 'tsp'), may hold values from -0.1875 to 0.1875
- adapter_place_table: int32 [64], replicated, may hold values from 0 to 63, as said below
- segment_adapter: int32 [512], P('dp'), may hold values from 0 to 63, as said below
- segment_live_count: int32 [512], P('dp'), may hold values from 1 to 128, as said below
Outputs:
- token_gradient: bfloat16 [65536, 8192], P('dp', 'tsp')
- down_grad: float32 [64, 64, 8192], P('dp', None, 'tsp')
- up_grad: float32 [64, 64, 1024], P('dp', None, 'tsp')
Inputs may be any that keep to these rules, and one draw needn't show every extreme that they name: A permutation: adapter a is held at place adapter_place_table[a], that is by the dp index adapter_place_table[a] // 2 as its entry adapter_place_table[a] % 2; the adapters' arrays and gradients are indexed by place. `segment_adapter`: the 16 segments of one dp index name at most one adapter held by any one dp index; an adapter may be named by several of them. `segment_live_count`: the live rows stand at the start of each segment; on every dp index some segment is full.
All inputs are finite; a program needn't handle non-finite values.
Results may differ from a plain program's by a relative error of at most 0.0034.
Values may be sent and summed in bfloat16 or wider, within the bound.
A program may use at most 128 MiB of HBM per device.

v0:
```python
import jax
import jax.numpy as jnp
from jax import lax
from jax.sharding import PartitionSpec as P

ADAPTER_SCALE = 2.0


def lookup(idents, mapping):
    matches = idents[:, None] == jnp.arange(mapping.shape[0], dtype=jnp.int32)[None, :]
    return jnp.sum(jnp.where(matches, mapping[None, :], 0), axis=1)


def on_device(
    tokens,
    cotangent,
    frozen_key_weight,
    adapter_down_weight,
    adapter_up_weight,
    adapter_place_table,
    segment_adapter,
    segment_live_count,
):
    dp_count = lax.axis_size("dp")
    places_per_device = adapter_down_weight.shape[0]
    rank_of_adapter = adapter_down_weight.shape[1]
    width_per_device = tokens.shape[1]
    key_dev = cotangent.shape[1]
    segments_per_device = segment_adapter.shape[0]
    segment_token_rows = tokens.shape[0] // segments_per_device
    adapter_places = lookup(segment_adapter, adapter_place_table)
    seg_owner = adapter_places // places_per_device
    seg_entry = adapter_places % places_per_device
    owner_hit = seg_owner[:, None] == jnp.arange(dp_count, dtype=jnp.int32)[None, :]
    wanted = jnp.max(jnp.where(owner_hit, seg_entry[:, None], -1), axis=0)
    incoming = lax.all_to_all(wanted[:, None], "dp", split_axis=0, concat_axis=0, tiled=True)[:, 0]
    serving_mesh = (
        incoming[:, None] == jnp.arange(places_per_device, dtype=jnp.int32)[None, :]
    ).astype(jnp.bfloat16)
    reply_down = jnp.einsum(
        "ap,phc->ahc", serving_mesh, adapter_down_weight, preferred_element_type=jnp.float32
    ).astype(jnp.bfloat16)
    reply_up = jnp.einsum(
        "hv,vun->hun", serving_mesh, adapter_up_weight, preferred_element_type=jnp.float32
    ).astype(jnp.bfloat16)
    fetched_down, fetched_up = (
        lax.all_to_all(reply_down, "dp", split_axis=0, concat_axis=0, tiled=True),
        lax.all_to_all(reply_up, "dp", split_axis=0, concat_axis=0, tiled=True),
    )
    picker = owner_hit.astype(jnp.bfloat16)
    segment_down_weight = jnp.einsum(
        "go,ord->grd", picker, fetched_down, preferred_element_type=jnp.float32
    ).astype(jnp.bfloat16)
    segment_up_weight = jnp.einsum(
        "go,ork->grk", picker, fetched_up, preferred_element_type=jnp.float32
    ).astype(jnp.bfloat16)
    seg_tokens = tokens.reshape(segments_per_device, segment_token_rows, width_per_device)
    seg_cotangent = cotangent.reshape(segments_per_device, segment_token_rows, key_dev)
    live_rows = (
        jnp.arange(segment_token_rows, dtype=jnp.int32)[None, :] < segment_live_count[:, None]
    ).astype(jnp.float32)
    partial_terms = jnp.concatenate(
        [
            jnp.einsum(
                "gtd,grd->gtr", seg_tokens, segment_down_weight, preferred_element_type=jnp.float32
            ),
            jnp.einsum(
                "gtk,grk->gtr", seg_cotangent, segment_up_weight, preferred_element_type=jnp.float32
            ),
        ],
        axis=2,
    )
    summed = lax.psum(partial_terms, "tsp")
    reduced_rows = (summed[:, :, :rank_of_adapter] * live_rows[:, :, None]).astype(jnp.bfloat16)
    gathered_weights = (summed[:, :, rank_of_adapter:] * live_rows[:, :, None]).astype(jnp.bfloat16)
    frozen_output = lax.dot_general(
        lax.all_gather(cotangent, "tsp", axis=1, tiled=True),
        frozen_key_weight,
        (((1,), (1,)), ((), ())),
        preferred_element_type=jnp.float32,
    )
    adapter_output = jnp.einsum(
        "wks,wsx->wkx", gathered_weights, segment_down_weight, preferred_element_type=jnp.float32
    )
    token_gradient = (
        frozen_output.reshape(segments_per_device, segment_token_rows, width_per_device)
        + ADAPTER_SCALE * adapter_output
    ) * live_rows[:, :, None]
    token_gradient = token_gradient.reshape(
        segments_per_device * segment_token_rows, width_per_device
    ).astype(jnp.bfloat16)
    gradient_scale = ADAPTER_SCALE / segment_token_rows
    segment_down_gradient = jnp.einsum(
        "upf,upb->ufb", gathered_weights, seg_tokens, preferred_element_type=jnp.float32
    )
    segment_up_gradient = jnp.einsum(
        "ija,ijn->ian", reduced_rows, seg_cotangent, preferred_element_type=jnp.float32
    )
    picker_f = owner_hit.astype(jnp.float32)
    slot_dgrad = (
        jnp.einsum("go,grd->ord", picker_f, segment_down_gradient, precision=lax.Precision.HIGHEST)
        * gradient_scale
    )
    slot_ugrad = (
        jnp.einsum("go,grk->ork", picker_f, segment_up_gradient, precision=lax.Precision.HIGHEST)
        * gradient_scale
    )
    slot_match = (wanted[:, None] == jnp.arange(places_per_device, dtype=jnp.int32)[None, :])[
        :, :, None, None
    ]
    dense_down = jnp.where(slot_match, slot_dgrad[:, None], 0.0).reshape(
        dp_count * places_per_device, rank_of_adapter, width_per_device
    )
    dense_up = jnp.where(slot_match, slot_ugrad[:, None], 0.0).reshape(
        dp_count * places_per_device, rank_of_adapter, key_dev
    )
    down_grad, up_grad = (
        lax.psum_scatter(dense_down, "dp", scatter_dimension=0, tiled=True),
        lax.psum_scatter(dense_up, "dp", scatter_dimension=0, tiled=True),
    )
    return (token_gradient, down_grad, up_grad)


def solution(mesh):
    placed = (
        P("dp", "tsp"),
        P("dp", "tsp"),
        P("tsp", None),
        P("dp", None, "tsp"),
        P("dp", None, "tsp"),
        P(),
        P("dp"),
        P("dp"),
    )
    return jax.shard_map(
        on_device,
        mesh=mesh,
        in_specs=placed,
        out_specs=(P("dp", "tsp"), P("dp", None, "tsp"), P("dp", None, "tsp")),
        check_vma=False,
    )
```

profile of v0, /device:TPU:2, one launch (start us, length us, event | category | flops | bytes accessed | tf_op | source)
XLA Modules:
  0.0 471.3 jit_solution(15498572598505192805)
XLA Ops:
  7.2 0.0 copy-start
  7.2 1.0 select_reduce_fusion.1
  8.2 0.1 select_reduce_fusion
  8.3 0.1 copy.57
  8.4 13.6 %all_to_all.19 = s32[32,1,1]{2,1,0:T(1,128)S(1)} all-to-all(s32[32,1,1]{2,1,0:T(1,128)S(1)} %copy.57), channel_id=1, replica_groups=mesh['dp'=32,'tsp'=8] {'dp'}, dimensions={0} | all-to-all | bytes 256 | tf_op jit(solution)/shard_map/all_to_all | solution.py:36
  22.0 0.7 reduce
  22.6 1.1 convolution_convert_fusion.1
  23.8 1.0 copy.63
  24.8 5.0 %all-to-all-start.2 = ((bf16[32,64,128]{2,1,0:T(8,128)(2,1)}), bf16[32,64,128]{2,1,0:T(8,128)(2,1)S(1)}, u32[]{:S(2)}, u32[]{:S(2)}) async-start(bf16[32,64,128]{2,1,0:T(8,128)(2,1)} %copy.63), calls=%async_computation.2 | async-start | bytes 1048576 | tf_op jit(solution)/shard_map/all_to_all | solution.py:48
  29.8 2.3 convolution_convert_fusion
  32.0 4.3 copy.59
  36.4 3.9 all-to-all-done.2
  40.2 5.9 %all-to-all-start.1 = ((bf16[32,64,1024]{2,1,0:T(8,128)(2,1)}), bf16[32,64,1024]{2,1,0:T(8,128)(2,1)}, u32[]{:S(2)}, u32[]{:S(2)}) async-start(bf16[32,64,1024]{2,1,0:T(8,128)(2,1)} %copy.59), calls=%async_computation.1 | async-start | bytes 8388608 | tf_op jit(solution)/shard_map/all_to_all | solution.py:47
  46.2 0.2 all-reduce.2.cloned.1.call-start
  46.4 0.4 convolution_convert_fusion.2
  46.8 0.4 convolution_bitcast_fusion
  47.3 50.4 %all-to-all-done.1 = bf16[32,64,1024]{2,1,0:T(8,128)(2,1)} async-done(((bf16[32,64,1024]{2,1,0:T(8,128)(2,1)}), bf16[32,64,1024]{2,1,0:T(8,128)(2,1)}, u32[]{:S(2)}, u32[]{:S(2)}) %all-to-all-start.1) | async-done | bytes 4194336 | tf_op jit(solution)/shard_map/all_to_all | solution.py:47
  97.7 6.9 %fusion.6 = bf16[16,64,1024]{2,0,1:T(8,128)(2,1)S(1)} fusion(bf16[32,64,1024]{2,1,0:T(8,128)(2,1)} %all-to-all-done.1, s32[16]{0:T(128)S(1)} %get-tuple-element.3), kind=kOutput, calls=%fused_computation.9 | convolution fusion | flops 68157952 | bytes 6291520 | tf_op jit(solution)/shard_map/go,ord->grd/dot_general | solution.py:51
  104.6 1.3 copy-done.1
  105.9 0.0 copy-done.3
  105.9 1.7 fusion.12
  107.6 1.1 pad_maximum_fusion
  108.7 0.0 all-reduce.2.cloned.1.call-update
  108.8 0.0 all-gather.2.cloned.1.call-start
  108.8 0.7 all-gather.2.cloned.1.call-update
  109.5 0.0 reduce-scatter.5.cloned.1.call-start
  109.6 0.1 iota_compare_fusion
  109.6 0.1 eq.76
  109.8 0.0 copy-done.7
  109.8 0.1 fusion.33
  109.8 75.4 %all-reduce.2.cloned.1.call-done = f32[16,128,128]{1,2,0:T(8,128)} async-done(((f32[16,128,128]{1,2,0:T(8,128)}), f32[16,128,128]{1,2,0:T(8,128)}) %all-reduce.2.cloned.1.call-update) | async-done | bytes 1048592 | tf_op jit(solution)/shard_map/psum | solution.py:73
  185.3 1.3 fusion.19
  186.6 0.9 convolution_multiply_fusion
  187.5 0.6 copy.70
  188.1 1.5 bitcast_select_fusion.1
  189.6 0.0 reduce-scatter.5.cloned.1.call-update
  189.7 0.3 reduce-scatter.3.cloned.1.call-start
  189.9 2.9 fusion.24
  192.8 6.1 %broadcast_multiply_fusion = f32[32,64,1024]{2,0,1:T(8,128)S(1)} fusion(f32[16,64,1024]{2,1,0:T(8,128)S(1)} %fusion.24, s32[16]{0:T(128)S(1)} %get-tuple-element.3), kind=kOutput, calls=%fused_computation.6 | convolution fusion | flops 404750848 | bytes 12582976 | tf_op jit(solution)/shard_map/go,grd->ord/dot_general | solution.py:101
  198.9 8.1 %copy.68 = f32[32,64,1024]{2,1,0:T(8,128)} copy(f32[32,64,1024]{2,0,1:T(8,128)S(1)} %broadcast_multiply_fusion) | data formatting | bytes 16777216 | tf_op jit(solution)/shard_map/mul | solution.py:101
  207.0 12.7 %bitcast_select_fusion = f32[64,64,1024]{2,1,0:T(8,128)} fusion(f32[32,64,1024]{2,1,0:T(8,128)} %copy.68, pred[64]{0:T(512)(128)(4,1)S(1)} %eq.76), kind=kLoop, calls=%fused_computation | loop fusion | flops 4194304 | bytes 25165888 | tf_op jit(solution)/shard_map/jit(_where)/select_n | solution.py:111
  219.7 0.0 reduce-scatter.3.cloned.1.call-update
  219.8 28.1 %all-gather.2.cloned.1.call-done = bf16[2048,1024]{1,0:T(8,128)(2,1)} async-done(((bf16[2048,128]{1,0:T(8,128)(2,1)}), bf16[2048,1024]{1,0:T(8,128)(2,1)}) %all-gather.2.cloned.1.call-update) | async-done | bytes 4194320 | tf_op jit(solution)/shard_map/all_gather | solution.py:77
  247.9 6.5 %fusion.42 = f32[2048,1024]{1,0:T(8,128)S(1)} fusion(bf16[2048,1024]{1,0:T(8,128)(2,1)} %all-gather.2.cloned.1.call-done, bf16[1024,1024]{1,0:T(8,128)(2,1)S(1)} %copy-done), kind=kOutput, calls=%fused_computation.53 | convolution fusion | flops 4294967296 | bytes 14680064 | tf_op jit(solution)/shard_map/dot_general | solution.py:76
  254.4 0.0 copy-done.2
  254.4 5.2 %multiply_convert_fusion = bf16[16,128,1024]{2,1,0:T(8,128)(2,1)} fusion(f32[16,128,1024]{2,1,0:T(8,128)S(1)} %bitcast.32, f32[16,128]{1,0:T(8,128)S(1)} %fusion.33, bf16[16,64,1024]{2,0,1:T(8,128)(2,1)S(1)} %copy-done.2, f32[16,128,128]{1,2,0:T(8,128)S(1)} %copy-done.6), kind=kOutput, calls=%fused_computation.1 | convolution fusion | flops 277086208 | bytes 15220736 | tf_op jit(solution)/shard_map/wks,wsx->wkx/dot_general | solution.py:82
  259.7 77.8 %reduce-scatter.5.cloned.1.call-done = f32[2,64,128]{2,1,0:T(8,128)} async-done(((f32[64,64,128]{2,1,0:T(8,128)}), f32[2,64,128]{2,1,0:T(8,128)}) %reduce-scatter.5.cloned.1.call-update) | async-done | bytes 65552 | tf_op jit(solution)/shard_map/reduce_scatter | solution.py:119
  337.5 127.2 %reduce-scatter.3.cloned.1.call-done = f32[2,64,1024]{2,1,0:T(8,128)} async-done(((f32[64,64,1024]{2,1,0:T(8,128)}), f32[2,64,1024]{2,1,0:T(8,128)}) %reduce-scatter.3.cloned.1.call-update) | async-done | bytes 524304 | tf_op jit(solution)/shard_map/reduce_scatter | solution.py:118
  (12 shorter events, 0.0 us)
Async XLA Ops:
  7.2 240.8 %copy-start = (bf16[1024,1024]{1,0:T(8,128)(2,1)S(1)}, bf16[1024,1024]{1,0:T(8,128)(2,1)}, u32[]{:S(2)}) copy-start(bf16[1024,1024]{1,0:T(8,128)(2,1)} %param.10) | copy-start | bytes 6291460
  24.8 15.5 %all-to-all-start.2 = ((bf16[32,64,128]{2,1,0:T(8,128)(2,1)}), bf16[32,64,128]{2,1,0:T(8,128)(2,1)S(1)}, u32[]{:S(2)}, u32[]{:S(2)}) async-start(bf16[32,64,128]{2,1,0:T(8,128)(2,1)} %copy.63), calls=%async_computation.2 | async-start | bytes 1048576 | tf_op jit(solution)/shard_map/all_to_all | solution.py:48
  36.4 10.4 %copy-start.4 = (bf16[2048,128]{1,0:T(8,128)(2,1)S(1)}, bf16[2048,128]{1,0:T(8,128)(2,1)}, u32[]{:S(2)}) copy-start(bf16[2048,128]{1,0:T(8,128)(2,1)} %param.9) | copy-start | bytes 1572868
  40.2 57.4 %all-to-all-start.1 = ((bf16[32,64,1024]{2,1,0:T(8,128)(2,1)}), bf16[32,64,1024]{2,1,0:T(8,128)(2,1)}, u32[]{:S(2)}, u32[]{:S(2)}) async-start(bf16[32,64,1024]{2,1,0:T(8,128)(2,1)} %copy.59), calls=%async_computation.1 | async-start | bytes 8388608 | tf_op jit(solution)/shard_map/all_to_all | solution.py:47
  46.2 139.1 %all-reduce.2.cloned.1.call-start = ((), (), s32[]{:S(2)}) async-start(), calls=%async_computation.6 | async-start | bytes 2097152 | tf_op jit(solution)/shard_map/psum | solution.py:73
  97.7 8.2 %copy-start.3 = (bf16[2048,1024]{1,0:T(8,128)(2,1)S(1)}, bf16[2048,1024]{1,0:T(8,128)(2,1)}, u32[]{:S(2)}) copy-start(bf16[2048,1024]{1,0:T(8,128)(2,1)} %param.8) | copy-start | bytes 12582916
  104.6 1.3 copy-start.1
  105.9 3.9 copy-start.7
  105.9 79.4 %copy-start.5 = (bf16[2048,128]{1,0:T(8,128)(2,1)S(1)}, bf16[2048,128]{1,0:T(8,128)(2,1)}, u32[]{:S(2)}) copy-start(bf16[2048,128]{1,0:T(8,128)(2,1)} %param.9) | copy-start | bytes 1572868
  108.8 139.1 %all-gather.2.cloned.1.call-start = ((), (), s32[]{:S(2)}) async-start(), calls=%async_computation.5 | async-start | bytes 4718592 | tf_op jit(solution)/shard_map/all_gather | solution.py:77
  109.5 228.0 %reduce-scatter.5.cloned.1.call-start = ((), (), s32[]{:S(2)}) async-start(), calls=%async_computation.8 | async-start | bytes 2162688 | tf_op jit(solution)/shard_map/reduce_scatter | solution.py:119
  186.6 3.4 copy-start.6
  189.7 275.1 %reduce-scatter.3.cloned.1.call-start = ((), (), s32[]{:S(2)}) async-start(), calls=%async_computation.7 | async-start | bytes 17301504 | tf_op jit(solution)/shard_map/reduce_scatter | solution.py:118
  247.9 6.5 %copy-start.2 = (bf16[16,64,1024]{2,0,1:T(8,128)(2,1)S(1)}, bf16[16,64,1024]{2,0,1:T(8,128)(2,1)}, u32[]{:S(2)}) copy-start(bf16[16,64,1024]{2,0,1:T(8,128)(2,1)} %copy-done.1) | copy-start | bytes 6291460
Sparse Core Ops, SparseCore 0:
  108.9 76.3 all-reduce.1
  187.0 60.8 all-gather.1
  252.3 85.1 reduce-scatter.4
  342.1 122.5 reduce-scatter.2
where the time goes:
time: 472 us; the launch traced here: 471 us
  waiting for transfers between devices  364 us (77%)
  matrix products  35.8 us (8%)
  other arithmetic  17.3 us (4%)
  local copies, waits for them, and re-layouts  15.6 us (3%)
  between operations  13.9 us (3%)
  blocking collectives  13.6 us (3%)
  starting transfers between devices  11.5 us (2%)
    reduce_scatter x1, waiting for transfers between devices, on_device(): lax.psum_scatter(dense_down, 'dp', scatter_dimension=0, tiled=True)  127 us
    reduce_scatter x1, waiting for transfers between devices, on_device(): lax.psum_scatter(dense_up, 'dp', scatter_dimension=0, tiled=True)  77.8 us
    psum x1, waiting for transfers between devices, on_device(): summed = lax.psum(partial_terms, 'tsp')  75.4 us
    all_to_all x1, waiting for transfers between devices, on_device(): lax.all_to_all(reply_down, 'dp', split_axis=0, concat_axis=0, tiled=True)  50.4 us
    all_gather x1, waiting for transfers between devices, on_device(): lax.all_gather(cotangent, 'tsp', axis=1, tiled=True)  28.1 us
    all_to_all x1, blocking collectives, on_device(): lax.all_to_all(wanted[:, None], 'dp', split_axis=0, concat_axis=0, tiled=...  13.6 us
    select_n x1, other arithmetic, on_device(): jnp.where(slot_match, slot_dgrad[:, None], 0.0)  12.7 us
  transfers between devices with their start and end apart: 6, of which 6 were waited for; matrix products, arithmetic and copies ran while one was open for 11% of the time, Pallas kernels for 0%

commit v1 on v0

--- a/solution.py
+++ b/solution.py
@@ -70,7 +70,7 @@
         ],
         axis=2,
     )
-    summed = lax.psum(partial_terms, "tsp")
+    summed = jnp.sum(lax.all_gather(partial_terms, "tsp"), axis=0)
     reduced_rows = (summed[:, :, :rank_of_adapter] * live_rows[:, :, None]).astype(jnp.bfloat16)
     gathered_weights = (summed[:, :, rank_of_adapter:] * live_rows[:, :, None]).astype(jnp.bfloat16)
     frozen_output = lax.dot_general(

time: 472 us -> 490 us (1.038)
  waiting for transfers between devices: 364 us -> 372 us
  local copies, waits for them, and re-layouts: 15.6 us -> 22 us
    all_gather x0 -> x1, waiting for transfers between devices: none -> 93.5 us  [on_device(): summed = jnp.sum(lax.all_gather(partial_terms, 'tsp'), axis=0)]
    psum x1 -> x0, waiting for transfers between devices: 75.4 us -> none  [on_device(): summed = lax.psum(partial_terms, 'tsp')]
    all_gather x1, waiting for transfers between devices: 28.1 us -> 19.4 us  [on_device(): lax.all_gather(cotangent, 'tsp', axis=1, tiled=True)]
  transfers between devices with their start and end apart: 6 -> 6, of which waited for: 6 -> 6; matrix products, arithmetic and copies ran while one was open for 11% -> 13% of each run, Pallas kernels for 0% -> 0%
where the time goes in v1:
time: 490 us
  waiting for transfers between devices  372 us (76%)
  matrix products  36.6 us (7%)
  local copies, waits for them, and re-layouts  22 us (4%)
  other arithmetic  20.1 us (4%)
  between operations  13.9 us (3%)
  blocking collectives  13.6 us (3%)
  starting transfers between devices  11.5 us (2%)
    reduce_scatter x1, waiting for transfers between devices, on_device(): lax.psum_scatter(dense_down, 'dp', scatter_dimension=0, tiled=True)  127 us
    all_gather x1, waiting for transfers between devices, on_device(): summed = jnp.sum(lax.all_gather(partial_terms, 'tsp'), axis=0)  93.5 us
    reduce_scatter x1, waiting for transfers between devices, on_device(): lax.psum_scatter(dense_up, 'dp', scatter_dimension=0, tiled=True)  77.6 us
    all_to_all x1, waiting for transfers between devices, on_device(): lax.all_to_all(reply_down, 'dp', split_axis=0, concat_axis=0, tiled=True)  49.6 us
    all_gather x1, waiting for transfers between devices, on_device(): lax.all_gather(cotangent, 'tsp', axis=1, tiled=True)  19.4 us
    all_to_all x1, blocking collectives, on_device(): lax.all_to_all(wanted[:, None], 'dp', split_axis=0, concat_axis=0, tiled=...  13.6 us
    select_n x1, other arithmetic, on_device(): jnp.where(slot_match, slot_dgrad[:, None], 0.0)  12.4 us
  transfers between devices with their start and end apart: 6, of which 6 were waited for; matrix products, arithmetic and copies ran while one was open for 13% of the time, Pallas kernels for 0%

profile of v1, /device:TPU:2, one launch (start us, length us, event | category | flops | bytes accessed | tf_op | source)
XLA Modules:
  0.0 489.7 jit_solution(4967920647770230533)
XLA Ops:
  7.2 1.0 select_reduce_fusion.1
  8.2 0.1 select_reduce_fusion
  8.3 0.1 copy.81
  8.4 13.6 %all_to_all.19 = s32[32,1,1]{2,1,0:T(1,128)S(1)} all-to-all(s32[32,1,1]{2,1,0:T(1,128)S(1)} %copy.81), channel_id=1, replica_groups=mesh['dp'=32,'tsp'=8] {'dp'}, dimensions={0} | all-to-all | bytes 256 | tf_op jit(solution)/shard_map/all_to_all | solution.py:36
  22.0 0.7 reduce
  22.6 1.1 convolution_convert_fusion.1
  23.8 1.0 copy.87
  24.8 5.0 %all-to-all-start.2 = ((bf16[32,64,128]{2,1,0:T(8,128)(2,1)}), bf16[32,64,128]{2,1,0:T(8,128)(2,1)S(1)}, u32[]{:S(2)}, u32[]{:S(2)}) async-start(bf16[32,64,128]{2,1,0:T(8,128)(2,1)} %copy.87), calls=%async_computation.2 | async-start | bytes 1048576 | tf_op jit(solution)/shard_map/all_to_all | solution.py:48
  29.8 2.3 convolution_convert_fusion
  32.0 4.3 copy.83
  36.4 3.9 all-to-all-done.2
  40.2 5.9 %all-to-all-start.1 = ((bf16[32,64,1024]{2,1,0:T(8,128)(2,1)}), bf16[32,64,1024]{2,1,0:T(8,128)(2,1)}, u32[]{:S(2)}, u32[]{:S(2)}) async-start(bf16[32,64,1024]{2,1,0:T(8,128)(2,1)} %copy.83), calls=%async_computation.1 | async-start | bytes 8388608 | tf_op jit(solution)/shard_map/all_to_all | solution.py:47
  46.2 0.2 all-gather.6.cloned.1.call-start
  46.4 0.4 convolution_convert_fusion.2
  46.8 1.3 convolution_bitcast_fusion
  48.1 49.6 %all-to-all-done.1 = bf16[32,64,1024]{2,1,0:T(8,128)(2,1)} async-done(((bf16[32,64,1024]{2,1,0:T(8,128)(2,1)}), bf16[32,64,1024]{2,1,0:T(8,128)(2,1)}, u32[]{:S(2)}, u32[]{:S(2)}) %all-to-all-start.1) | async-done | bytes 4194336 | tf_op jit(solution)/shard_map/all_to_all | solution.py:47
  97.7 6.9 %fusion.6 = bf16[16,64,1024]{2,0,1:T(8,128)(2,1)S(1)} fusion(bf16[32,64,1024]{2,1,0:T(8,128)(2,1)} %all-to-all-done.1, s32[16]{0:T(128)S(1)} %get-tuple-element.5), kind=kOutput, calls=%fused_computation.9 | convolution fusion | flops 68157952 | bytes 6291520 | tf_op jit(solution)/shard_map/go,ord->grd/dot_general | solution.py:51
  104.6 1.3 copy-done.1
  105.9 1.7 fusion.12
  107.6 0.1 pad_maximum_fusion
  107.7 1.4 copy.90
  109.1 0.0 all-gather.6.cloned.1.call-update
  109.1 0.0 all-gather.4.cloned.1.call-start
  109.2 0.7 all-gather.4.cloned.1.call-update
  109.9 0.0 reduce-scatter.5.cloned.1.call-start
  109.9 0.1 iota_compare_fusion
  110.0 0.1 eq.76
  110.1 0.1 fusion.28
  110.2 93.5 %all-gather.6.cloned.1.call-done = f32[128,128,128]{2,1,0:T(8,128)} async-done(((f32[16,128,128]{2,1,0:T(8,128)}), f32[128,128,128]{2,1,0:T(8,128)}) %all-gather.6.cloned.1.call-update) | async-done | bytes 8388624 | tf_op jit(solution)/shard_map/all_gather | solution.py:73
  203.8 4.2 reduce_sum.19
  207.9 1.7 fusion.37
  209.6 1.5 copy.99
  211.2 1.3 fusion.17
  212.5 0.9 convolution_multiply_fusion
  213.4 0.6 copy.97
  214.0 1.5 bitcast_select_fusion.1
  215.5 0.0 reduce-scatter.5.cloned.1.call-update
  215.6 0.3 reduce-scatter.3.cloned.1.call-start
  215.8 1.6 copy.98
  217.4 2.9 fusion.21
  220.3 6.1 %broadcast_multiply_fusion = f32[32,64,1024]{2,0,1:T(8,128)S(1)} fusion(f32[16,64,1024]{2,1,0:T(8,128)S(1)} %fusion.21, s32[16]{0:T(128)S(1)} %get-tuple-element.5), kind=kOutput, calls=%fused_computation.6 | convolution fusion | flops 404750848 | bytes 12582976 | tf_op jit(solution)/shard_map/go,grd->ord/dot_general | solution.py:101
  226.4 8.4 %copy.94 = f32[32,64,1024]{2,1,0:T(8,128)} copy(f32[32,64,1024]{2,0,1:T(8,128)S(1)} %broadcast_multiply_fusion) | data formatting | bytes 16777216 | tf_op jit(solution)/shard_map/mul | solution.py:101
  234.7 12.4 %bitcast_select_fusion = f32[64,64,1024]{2,1,0:T(8,128)} fusion(f32[32,64,1024]{2,1,0:T(8,128)} %copy.94, pred[64]{0:T(512)(128)(4,1)S(1)} %eq.76), kind=kLoop, calls=%fused_computation | loop fusion | flops 4194304 | bytes 25165888 | tf_op jit(solution)/shard_map/jit(_where)/select_n | solution.py:111
  247.2 19.4 %all-gather.4.cloned.1.call-done = bf16[2048,1024]{1,0:T(8,128)(2,1)} async-done(((bf16[2048,128]{1,0:T(8,128)(2,1)}), bf16[2048,1024]{1,0:T(8,128)(2,1)}) %all-gather.4.cloned.1.call-update) | async-done | bytes 4194320 | tf_op jit(solution)/shard_map/all_gather | solution.py:77
  266.6 6.5 %fusion.38 = f32[2048,1024]{1,0:T(8,128)S(1)} fusion(bf16[2048,1024]{1,0:T(8,128)(2,1)} %all-gather.4.cloned.1.call-done, bf16[1024,1024]{1,0:T(8,128)(2,1)S(1)} %copy-done), kind=kOutput, calls=%fused_computation.52 | convolution fusion | flops 4294967296 | bytes 14680064 | tf_op jit(solution)/shard_map/dot_general | solution.py:76
  273.1 5.2 %multiply_convert_fusion = bf16[16,128,1024]{2,1,0:T(8,128)(2,1)} fusion(f32[16,128,1024]{2,1,0:T(8,128)S(1)} %bitcast.33, f32[16,128]{1,0:T(8,128)S(1)} %fusion.28, bf16[16,64,1024]{2,0,1:T(8,128)(2,1)S(1)} %copy-done.2, f32[16,128,64]{1,2,0:T(8,128)S(1)} %copy.98), kind=kOutput, calls=%fused_computation.1 | convolution fusion | flops 277086208 | bytes 15212544 | tf_op jit(solution)/shard_map/wks,wsx->wkx/dot_general | solution.py:82
  278.3 77.6 %reduce-scatter.5.cloned.1.call-done = f32[2,64,128]{2,1,0:T(8,128)} async-done(((f32[64,64,128]{2,1,0:T(8,128)}), f32[2,64,128]{2,1,0:T(8,128)}) %reduce-scatter.5.cloned.1.call-update) | async-done | bytes 65552 | tf_op jit(solution)/shard_map/reduce_scatter | solution.py:119
  355.9 127.2 %reduce-scatter.3.cloned.1.call-done = f32[2,64,1024]{2,1,0:T(8,128)} async-done(((f32[64,64,1024]{2,1,0:T(8,128)}), f32[2,64,1024]{2,1,0:T(8,128)}) %reduce-scatter.3.cloned.1.call-update) | async-done | bytes 524304 | tf_op jit(solution)/shard_map/reduce_scatter | solution.py:118
  (15 shorter events, 0.1 us)
Async XLA Ops:
  7.2 259.4 %copy-start = (bf16[1024,1024]{1,0:T(8,128)(2,1)S(1)}, bf16[1024,1024]{1,0:T(8,128)(2,1)}, u32[]{:S(2)}) copy-start(bf16[1024,1024]{1,0:T(8,128)(2,1)} %param.10) | copy-start | bytes 6291460
  24.8 15.5 %all-to-all-start.2 = ((bf16[32,64,128]{2,1,0:T(8,128)(2,1)}), bf16[32,64,128]{2,1,0:T(8,128)(2,1)S(1)}, u32[]{:S(2)}, u32[]{:S(2)}) async-start(bf16[32,64,128]{2,1,0:T(8,128)(2,1)} %copy.87), calls=%async_computation.2 | async-start | bytes 1048576 | tf_op jit(solution)/shard_map/all_to_all | solution.py:48
  36.4 10.4 %copy-start.4 = (bf16[2048,128]{1,0:T(8,128)(2,1)S(1)}, bf16[2048,128]{1,0:T(8,128)(2,1)}, u32[]{:S(2)}) copy-start(bf16[2048,128]{1,0:T(8,128)(2,1)} %param.9) | copy-start | bytes 1572868
  40.2 57.4 %all-to-all-start.1 = ((bf16[32,64,1024]{2,1,0:T(8,128)(2,1)}), bf16[32,64,1024]{2,1,0:T(8,128)(2,1)}, u32[]{:S(2)}, u32[]{:S(2)}) async-start(bf16[32,64,1024]{2,1,0:T(8,128)(2,1)} %copy.83), calls=%async_computation.1 | async-start | bytes 8388608 | tf_op jit(solution)/shard_map/all_to_all | solution.py:47
  46.2 157.6 %all-gather.6.cloned.1.call-start = ((), (), s32[]{:S(2)}) async-start(), calls=%async_computation.8 | async-start | bytes 9437184 | tf_op jit(solution)/shard_map/all_gather | solution.py:73
  97.7 8.2 %copy-start.3 = (bf16[2048,1024]{1,0:T(8,128)(2,1)S(1)}, bf16[2048,1024]{1,0:T(8,128)(2,1)}, u32[]{:S(2)}) copy-start(bf16[2048,1024]{1,0:T(8,128)(2,1)} %param.8) | copy-start | bytes 12582916
  104.6 1.3 copy-start.1
  104.6 3.1 copy-start.5
  107.6 2.5 copy-start.6
  109.1 157.4 %all-gather.4.cloned.1.call-start = ((), (), s32[]{:S(2)}) async-start(), calls=%async_computation.5 | async-start | bytes 4718592 | tf_op jit(solution)/shard_map/all_gather | solution.py:77
  109.9 246.0 %reduce-scatter.5.cloned.1.call-start = ((), (), s32[]{:S(2)}) async-start(), calls=%async_computation.7 | async-start | bytes 2162688 | tf_op jit(solution)/shard_map/reduce_scatter | solution.py:119
  215.6 267.6 %reduce-scatter.3.cloned.1.call-start = ((), (), s32[]{:S(2)}) async-start(), calls=%async_computation.6 | async-start | bytes 17301504 | tf_op jit(solution)/shard_map/reduce_scatter | solution.py:118
  266.6 6.5 %copy-start.2 = (bf16[16,64,1024]{2,0,1:T(8,128)(2,1)S(1)}, bf16[16,64,1024]{2,0,1:T(8,128)(2,1)}, u32[]{:S(2)}) copy-start(bf16[16,64,1024]{2,0,1:T(8,128)(2,1)} %copy-done.1) | copy-start | bytes 6291460
Sparse Core Ops, SparseCore 0:
  109.3 94.4 all-gather.5
  205.5 61.0 all-gather.3
  271.0 84.9 reduce-scatter.4
  360.6 122.5 reduce-scatter.2
